TPU v7x, 32 devices: a whole 2x2x4 slice. The times are simulated.
32 devices in a mesh: groups: 2 (over y), seq: 4 (over z), head: 2 (over x), rep: 2 (over core).
Axes of the slice: x: 2, y: 2, z: 4, core: 2. Of those that a mesh axis runs over, the one named last changes fastest.
Arguments:
- book_tokens: bfloat16 [16384, 1024], P(('groups', 'seq', 'rep')), parts along dimension 0, may hold values from -6 to 6
- norm_gain: float32 [1024], replicated, may hold values from 0.1 to 1.9
- query_weight: bfloat16 [1024, 1024], P(None, 'head'), may hold values from -0.1875 to 0.1875
- key_weight: bfloat16 [1024, 1024], P(None, 'head'), may hold values from -0.1875 to 0.1875
- value_weight: bfloat16 [1024, 1024], P(None, 'head'), may hold values from -0.1875 to 0.1875
- proj_weight: bfloat16 [1024, 4096], P(None, 'head'), may hold values from -0.75 to 0.75
- dual_gains: float32 [4, 1024], P(None, 'head'), may hold values from 0.1 to 1.9
- out_weight: bfloat16 [1024, 1024], P(None, 'head'), may hold values from -1.5 to 1.5
- span_bounds: int32 [128, 2], P('groups'), parts along dimension 0, may hold values from 0 to 8192, as said below
Outputs:
- attended: bfloat16 [16384, 1024], P(('groups', 'seq', 'rep'), 'head'), parts along dimension 0
- pooled: float32 [128, 1024], P(('groups', 'seq', 'rep'), 'head'), parts along dimension 0
There are 2 independent parts, one for each index of `groups`. A program takes and returns all parts, laid end to end along the dimension named above; an argument that names none is the same for every part. Nothing has to cross between parts.
Inputs may be any that keep to these rules, and one draw needn't show every extreme that they name: `span_bounds`: each span lies inside the book and holds 1 to 512 tokens; spans may intersect and come in any order; the longest holds exactly 512 tokens.
All inputs are finite; a program needn't handle non-finite values.
Results may differ from a plain program's by a relative error of at most 0.023.
Values may be sent and summed in bfloat16 or wider, within the bound.
No kernel may reach another device: no remote copies, remote signals or barrier semaphores. Data moves between devices by JAX's collectives and lax.ppermute only.
A program may use at most 64 MiB of HBM per device.

v0:
```python
import jax
import jax.numpy as jnp
from jax import lax
from jax.sharding import PartitionSpec as P

DH = 64
R = 256
SEG = 128
softcap = 5.0
epsilon = 1e-05


def with_halo(cells, sides, width):
    for axis, dim in sides:
        count = lax.axis_size(axis)
        ends = count - 1
        head = lax.slice_in_dim(cells, 0, width, axis=dim)
        tail = lax.slice_in_dim(cells, cells.shape[dim] - width, cells.shape[dim], axis=dim)
        cells = jnp.concatenate(
            [
                lax.ppermute(tail, axis, [(i, (i + 1) % count) for i in range(ends)]),
                cells,
                lax.ppermute(head, axis, [((i + 1) % count, i) for i in range(ends)]),
            ],
            axis=dim,
        )
    return cells


def normalize(values, gain_row):
    centre = jnp.mean(values, axis=-1, keepdims=True)
    spread = jnp.mean(jnp.square(values - centre), axis=-1, keepdims=True)
    return (values - centre) * lax.rsqrt(spread + epsilon) * gain_row


def capped(values):
    return softcap * jnp.tanh(values / softcap)


def finish(total_numer, gain_rows):
    land_keys = normalize(total_numer[:, :, :DH], gain_rows[2][:, None, :])
    land_values = normalize(total_numer[:, :, DH:], gain_rows[3][:, None, :])
    return jnp.concatenate([land_keys, land_values], axis=-1).astype(jnp.bfloat16)


def per_device(
    book_tokens,
    norm_gain,
    query_weight,
    key_weight,
    value_weight,
    proj_weight,
    dual_gains,
    out_weight,
    span_bounds,
):
    tok_rows = book_tokens.shape[0]
    seq_devices = lax.axis_size(("seq", "rep"))
    seq_index = lax.axis_index(("seq", "rep"))
    first_row = seq_index * tok_rows
    length = tok_rows * seq_devices
    head_local = query_weight.shape[1] // DH
    normed = normalize(book_tokens.astype(jnp.float32), norm_gain).astype(jnp.bfloat16)
    queries = jnp.dot(normed, query_weight, preferred_element_type=jnp.float32).astype(jnp.bfloat16)
    queries = queries.reshape(tok_rows, head_local, DH)
    key_raw = jnp.dot(normed, key_weight, preferred_element_type=jnp.float32).reshape(
        tok_rows, head_local, DH
    )
    value_raw = jnp.dot(normed, value_weight, preferred_element_type=jnp.float32).reshape(
        tok_rows, head_local, DH
    )
    gain_rows = dual_gains.reshape(4, head_local, DH)
    near_pairs = jnp.concatenate(
        [normalize(key_raw, gain_rows[0]), normalize(value_raw, gain_rows[1])], axis=-1
    )
    near_pairs = near_pairs.astype(jnp.bfloat16)
    raw_pairs = jnp.concatenate([key_raw, value_raw], axis=-1).astype(jnp.bfloat16)
    logits = jnp.dot(normed, proj_weight, preferred_element_type=jnp.float32)
    proj_weights = jnp.exp(capped(logits)).astype(jnp.bfloat16).reshape(tok_rows, head_local, R)
    numerator = jnp.einsum(
        "nhr,nhe->hre", proj_weights, raw_pairs, preferred_element_type=jnp.float32
    )
    flat_pairs = near_pairs.reshape(tok_rows, head_local * 2 * DH)
    padded = with_halo(flat_pairs, ((("seq", "rep"), 0),), SEG // 2)
    segments = tok_rows // SEG
    blocks = padded.reshape(segments + 1, SEG, head_local, 2 * DH)
    window = jnp.concatenate([blocks[:-1], blocks[1:]], axis=1)
    position = (
        first_row + jnp.arange(segments)[:, None] * SEG + jnp.arange(2 * SEG)[None, :] - SEG // 2
    )
    inside = (position >= 0) & (position < length)
    query_blocks = queries.reshape(segments, SEG, head_local, DH)
    near_scores = jnp.einsum(
        "sqhd,skhd->shqk", query_blocks, window[..., :DH], preferred_element_type=jnp.float32
    )
    near_exp = jnp.where(inside[:, None, None, :], jnp.exp(capped(near_scores * DH ** (-0.5))), 0.0)
    total_numer = lax.psum(numerator.astype(jnp.bfloat16), ("seq", "rep")).astype(jnp.float32)
    land_pairs = finish(total_numer, gain_rows)
    far_scores = jnp.einsum(
        "sqhd,hrd->shqr", query_blocks, land_pairs[..., :DH], preferred_element_type=jnp.float32
    )
    far_exp = jnp.exp(capped(far_scores * DH ** (-0.5)))
    summed = jnp.sum(near_exp, axis=-1, keepdims=True) + jnp.sum(far_exp, axis=-1, keepdims=True)
    near_probs = (near_exp / summed).astype(jnp.bfloat16)
    far_probs = (far_exp / summed).astype(jnp.bfloat16)
    output = jnp.einsum(
        "shqk,skhd->sqhd", near_probs, window[..., DH:], preferred_element_type=jnp.float32
    )
    output = output + jnp.einsum(
        "shqr,hrd->sqhd", far_probs, land_pairs[..., DH:], preferred_element_type=jnp.float32
    )
    heads_out = output.astype(jnp.bfloat16).reshape(tok_rows, head_local * DH)
    projected = jnp.dot(
        lax.all_gather(heads_out, "head", axis=1, tiled=True),
        out_weight,
        preferred_element_type=jnp.float32,
    )
    attended = projected.astype(jnp.bfloat16)
    span_start = span_bounds[:, 0]
    span_end = span_bounds[:, 1]
    position_rows = first_row + jnp.arange(tok_rows)
    member = (position_rows[None, :] >= span_start[:, None]) & (
        position_rows[None, :] < span_end[:, None]
    )
    partial_sums = jnp.dot(
        member.astype(jnp.bfloat16), attended, preferred_element_type=jnp.float32
    )
    own_sums = lax.psum_scatter(
        partial_sums.astype(jnp.bfloat16), ("seq", "rep"), scatter_dimension=0, tiled=True
    ).astype(jnp.float32)
    span_rows = own_sums.shape[0]
    own_bounds = lax.dynamic_slice_in_dim(span_bounds, seq_index * span_rows, span_rows, 0)
    own_counts = (own_bounds[:, 1] - own_bounds[:, 0]).astype(jnp.float32)
    pooled = own_sums / own_counts[:, None]
    return (attended, pooled)


def solution(mesh):
    placed = (
        P(("groups", "seq", "rep"), None),
        P(),
        P(None, "head"),
        P(None, "head"),
        P(None, "head"),
        P(None, "head"),
        P(None, "head"),
        P(None, "head"),
        P("groups", None),
    )
    return jax.shard_map(
        per_device,
        mesh=mesh,
        in_specs=placed,
        out_specs=(P(("groups", "seq", "rep"), "head"), P(("groups", "seq", "rep"), "head")),
        check_vma=False,
    )
```

profile of v0, /device:TPU:0, one launch (start us, length us, event | category | flops | bytes accessed | tf_op | source)
XLA Modules:
  0.0 200.5 jit_solution(12161471431930354215)
XLA Ops:
  7.2 2.1 %convert_reduce_fusion = f32[1024]{0:T(1024)S(1)} fusion(bf16[1024,1024]{1,0:T(8,128)(2,1)} %param.9), kind=kLoop, calls=%fused_computation.9 | loop fusion | flops 2096128 | bytes 2101248 | tf_op jit(solution)/shard_map/reduce_sum | solution.py:31
  10.9 2.3 %bitcast_convert_fusion = (bf16[1024,8,64]{0,2,1:T(8,128)(2,1)}, f32[1024,512]{0,1:T(8,128)S(1)}) fusion(bf16[1024,1024]{1,0:T(8,128)(2,1)S(1)} %fusion.6, bf16[1024,512]{1,0:T(8,128)(2,1)S(1)} %copy-done), kind=kOutput, calls=%fused_computation.34 | convolution fusion | flops 1074266112 | bytes 6291456 | tf_op jit(solution)/shard_map/dot_general | solution.py:69
  14.4 2.3 %bitcast_convert_fusion.1 = (bf16[1024,8,64]{0,2,1:T(8,128)(2,1)}, f32[1024,512]{0,1:T(8,128)S(1)}) fusion(bf16[1024,1024]{1,0:T(8,128)(2,1)S(1)} %fusion.6, bf16[1024,512]{1,0:T(8,128)(2,1)S(1)} %copy-done.15), kind=kOutput, calls=%fused_computation.37 | convolution fusion | flops 1074266112 | bytes 6291456 | tf_op jit(solution)/shard_map/dot_general | solution.py:66
  18.3 2.2 %multiply_multiply_fusion = (bf16[1024,8,64]{0,2,1:T(8,128)(2,1)S(1)}, bf16[1024,8,64]{0,2,1:T(8,128)(2,1)S(1)}) fusion(f32[1024,512]{0,1:T(8,128)S(1)} %get-tuple-element.17, f32[8,64]{1,0:T(8,128)S(1)} %mul.128, f32[1024,8]{0,1:T(8,128)S(1)} %add_rsqrt_fusion, f32[1024,8]{0,1:T(8,128)S(1)} %broadcast_multiply_fusion, f32[8,64]{1,0:T(8,128)S(1)} %mul.123, ...), kind=kLoop, calls=%fused_computation.40 | loop fusion | flops 4194304 | bytes 6426624 | tf_op jit(solution)/shard_map/mul | solution.py:33
  21.0 2.4 %collective-permute-start = (bf16[64,1024]{1,0:T(8,128)(2,1)S(1)}, bf16[64,1024]{1,0:T(8,128)(2,1)S(1)}, u32[]{:S(2)}, u32[]{:S(2)}) collective-permute-start(bf16[64,1024]{1,0:T(8,128)(2,1)S(1)} %copy.38), channel_id=1, source_target_pairs={{0,1},{1,4},{4,5},{5,8},{8,9},{9,12},{12,13},{2,3},{3,6},{6,7},{7,... | collective-permute-start | bytes 393224 | tf_op jit(solution)/shard_map/ppermute | solution.py:21
  25.6 9.9 %exponential_convert_fusion = bf16[1024,2048]{1,0:T(8,128)(2,1)} fusion(bf16[1024,1024]{1,0:T(8,128)(2,1)} %copy-done.6, bf16[1024,2048]{1,0:T(8,128)(2,1)} %param.14), kind=kOutput, calls=%fused_computation.5 | convolution fusion | flops 4301258752 | bytes 10485760 | tf_op jit(solution)/shard_map/dot_general | solution.py:78
  35.6 6.5 %copy.58 = bf16[1024,2048]{0,1:T(8,128)(2,1)} copy(bf16[1024,2048]{1,0:T(8,128)(2,1)} %exponential_convert_fusion) | data formatting | bytes 8388608 | tf_op jit(solution)/shard_map/reshape | solution.py:79
  42.1 4.5 %fusion.23 = bf16[8,256,128]{2,1,0:T(8,128)(2,1)} fusion(bf16[1024,8,256]{0,2,1:T(8,128)(2,1)} %bitcast.78, bf16[1024,8,64]{0,2,1:T(8,128)(2,1)S(1)} %copy-done.17, bf16[1024,8,64]{0,2,1:T(8,128)(2,1)} %get-tuple-element.18), kind=kOutput, calls=%fused_computation.46 | convolution fusion | flops 541327360 | bytes 6815744 | tf_op jit(solution)/shard_map/nhr,nhe->hre/dot_general | solution.py:80
  46.9 2.6 %copy.39 = bf16[1024,1024]{1,0:T(8,128)(2,1)} copy(bf16[1024,1024]{0,1:T(8,128)(2,1)S(1)} %bitcast.75) | data formatting | bytes 4194304 | tf_op jit(solution)/shard_map/convert_element_type | solution.py:76
  49.5 3.1 %convolution_convert_fusion.1 = bf16[1024,512]{1,0:T(8,128)(2,1)S(1)} fusion(bf16[1024,1024]{1,0:T(8,128)(2,1)} %copy-done.6, bf16[1024,512]{1,0:T(8,128)(2,1)} %param.11), kind=kOutput, calls=%fused_computation.45 | convolution fusion | flops 1074266112 | bytes 4194304 | tf_op jit(solution)/shard_map/dot_general | solution.py:64
  52.6 2.1 %reshape.140 = bf16[8,128,8,64]{3,2,1,0:T(8,128)(2,1)} reshape(bf16[1024,512]{1,0:T(8,128)(2,1)S(1)} %convolution_convert_fusion.1) | data formatting | bytes 2097152 | tf_op jit(solution)/shard_map/reshape;reshape | solution.py:92
  54.7 2.4 %copy.45 = bf16[8,128,8,64]{1,3,2,0:T(8,128)(2,1)S(1)} copy(bf16[8,128,8,64]{3,2,1,0:T(8,128)(2,1)} %reshape.140) | data formatting | bytes 2097152 | tf_op jit(solution)/shard_map/reshape;reshape | solution.py:92
  59.3 2.0 copy.64
  61.2 4.3 %copy.42 = bf16[8,128,8,128]{1,3,2,0:T(8,128)(2,1)} copy(bf16[8,128,8,128]{3,2,1,0:T(8,128)(2,1)} %bitcast.76) | data formatting | bytes 4194304 | tf_op jit(solution)/shard_map/slice | solution.py:87
  65.5 1.9 copy.65
  67.5 4.3 %copy.43 = bf16[8,128,8,128]{1,3,2,0:T(8,128)(2,1)} copy(bf16[8,128,8,128]{3,2,1,0:T(8,128)(2,1)} %bitcast.77) | data formatting | bytes 4194304 | tf_op jit(solution)/shard_map/slice | solution.py:87
  71.7 7.5 %fusion.1 = (f32[8,8,128]{2,1,0:T(8,128)S(1)}, f32[8,8,128,256]{3,2,1,0:T(8,128)}) fusion(pred[8,256]{1,0:T(8,128)(4,1)S(1)} %fusion.45, bf16[8,128,8,64]{1,3,2,0:T(8,128)(2,1)S(1)} %copy.45, bf16[8,128,8,128]{1,3,2,0:T(8,128)(2,1)} %copy.43, bf16[8,128,8,128]{1,3,2,0:T(8,128)(2,1)S(1)} %copy-done.7), kind=kOutput, calls=%fused_computation.7 | convolution fusion | flops 281010176 | bytes 13666304 | tf_op jit(solution)/shard_map/sqhd,skhd->shqk/dot_general | solution.py:93
  79.2 28.3 %all-reduce.2.cloned.1.call-done = bf16[8,256,128]{2,1,0:T(8,128)(2,1)} async-done(((bf16[8,256,128]{2,1,0:T(8,128)(2,1)}), bf16[8,256,128]{2,1,0:T(8,128)(2,1)}) %all-reduce.2.cloned.1.call-update) | async-done | bytes 524304 | tf_op jit(solution)/shard_map/psum | solution.py:97
  111.2 3.9 %bitcast_reduce_fusion = (f32[8,8,128]{2,1,0:T(8,128)S(1)}, f32[8,256,8,128]{1,3,0,2:T(8,128)S(1)}) fusion(bf16[8,128,8,64]{1,3,2,0:T(8,128)(2,1)S(1)} %copy-done.10, f32[8,256,128]{2,1,0:T(8,128)S(1)} %convert_element_type.57, f32[8,64]{1,0:T(8,128)S(1)} %mul.138, f32[8,256]{1,0:T(8,128)S(1)} %add_rsqrt_fusion.3, f32[8,256]{1,0:T(8,128)S(1)} %get-tuple-element.25), kind=kOutput, calls=%fused_computation.1 | convolution fusion | flops 275243008 | bytes 10536960 | tf_op jit(solution)/shard_map/sqhd,hrd->shqr/dot_general | solution.py:99
  115.2 5.2 %fusion.8 = f32[8,64,8,128]{3,1,0,2:T(8,128)S(1)} fusion(f32[8,256,8,128]{1,3,0,2:T(8,128)S(1)} %get-tuple-element.23, f32[8,8,128]{2,1,0:T(8,128)S(1)} %add.118, f32[8,256,128]{2,1,0:T(8,128)S(1)} %convert_element_type.57, f32[8,64]{1,0:T(8,128)S(1)} %mul.144, f32[8,256]{1,0:T(8,128)S(1)} %add_rsqrt_fusion.2, f32[8,256]{1,0:T(8,128)S(1)} %get-tuple-element.24), kind=kOutput, calls=%fused_computation.19 | convolution fusion | flops 277348352 | bytes 11585536 | tf_op jit(solution)/shard_map/shqr,hrd->sqhd/dot_general | solution.py:109
  120.4 3.8 %fusion.20 = bf16[8,128,8,64]{1,3,2,0:T(8,128)(2,1)S(1)} fusion(f32[8,64,8,128]{3,1,0,2:T(8,128)S(1)} %fusion.8, f32[8,8,128,256]{3,2,1,0:T(8,128)S(1)} %bitcast.84, f32[8,8,128]{2,1,0:T(8,128)S(1)} %add.118, pred[8,256]{1,0:T(8,128)(4,1)S(1)} %fusion.45, bf16[8,128,8,128]{1,3,2,0:T(8,128)(2,1)S(1)} %copy-done.7, bf16[8,128,8,128]{1,3,2,0:T(8,128)(2,1)S(1)} %copy-done.8), kind=kOutput, calls=%fused_computation.33 | convolution fusion | flops 284164096 | bytes 15763456 | tf_op jit(solution)/shard_map/shqk,skhd->sqhd/dot_general | solution.py:106
  126.3 32.1 %all-gather.2.cloned.1.call-done = bf16[1024,1024]{0,1:T(8,128)(2,1)} async-done(((bf16[1024,512]{0,1:T(8,128)(2,1)}), bf16[1024,1024]{0,1:T(8,128)(2,1)}) %all-gather.2.cloned.1.call-update) | async-done | bytes 2097168 | tf_op jit(solution)/shard_map/all_gather | solution.py:114
  158.4 3.0 %convolution_convert_fusion = bf16[1024,512]{1,0:T(8,128)(2,1)S(1)} fusion(bf16[1024,1024]{0,1:T(8,128)(2,1)} %all-gather.2.cloned.1.call-done, bf16[1024,512]{1,0:T(8,128)(2,1)S(1)} %copy-done.16), kind=kOutput, calls=%fused_computation.44 | convolution fusion | flops 1074266112 | bytes 4194304 | tf_op jit(solution)/shard_map/dot_general | solution.py:113
  162.4 30.2 %reduce-scatter.2.cloned.1.call-done = bf16[8,512]{1,0:T(8,128)(2,1)} async-done(((bf16[64,512]{1,0:T(8,128)(2,1)}), bf16[8,512]{1,0:T(8,128)(2,1)}) %reduce-scatter.2.cloned.1.call-update) | async-done | bytes 8208 | tf_op jit(solution)/shard_map/reduce_scatter | solution.py:128
  (89 shorter events, 17.6 us)
Async XLA Ops:
  7.2 3.7 %copy-start = (bf16[1024,512]{1,0:T(8,128)(2,1)S(1)}, bf16[1024,512]{1,0:T(8,128)(2,1)}, u32[]{:S(2)}) copy-start(bf16[1024,512]{1,0:T(8,128)(2,1)} %param.13) | copy-start | bytes 3145732
  7.2 2.3 %copy-start.2 = (bf16[1024,1024]{1,0:T(8,128)(2,1)S(1)}, bf16[1024,1024]{1,0:T(8,128)(2,1)}, u32[]{:S(2)}) copy-start(bf16[1024,1024]{1,0:T(8,128)(2,1)} %param.9) | copy-start | bytes 6291460
  7.2 3.0 %copy-start.13 = (f32[1024]{0:T(1024)S(1)}, f32[1024]{0:T(1024)}, u32[]{:S(2)}) copy-start(f32[1024]{0:T(1024)} %param.10) | copy-start | bytes 12292
  7.2 100.3 %all-reduce.2.cloned.1.call-start = ((), (), s32[]{:S(2)}) async-start(), calls=%async_computation.1 | async-start | bytes 1048576 | tf_op jit(solution)/shard_map/psum | solution.py:97
  10.9 2.9 %copy-start.6 = (bf16[1024,1024]{1,0:T(8,128)(2,1)}, bf16[1024,1024]{1,0:T(8,128)(2,1)S(1)}, u32[]{:S(2)}) copy-start(bf16[1024,1024]{1,0:T(8,128)(2,1)S(1)} %fusion.6) | copy-start | bytes 6291460
  16.7 1.4 copy-start.3
  16.7 1.4 copy-start.12
  21.0 36.3 %collective-permute-start = (bf16[64,1024]{1,0:T(8,128)(2,1)S(1)}, bf16[64,1024]{1,0:T(8,128)(2,1)S(1)}, u32[]{:S(2)}, u32[]{:S(2)}) collective-permute-start(bf16[64,1024]{1,0:T(8,128)(2,1)S(1)} %copy.38), channel_id=1, source_target_pairs={{0,1},{1,4},{4,5},{5,8},{8,9},{9,12},{12,13},{2,3},{3,6},{6,7},{7,... | collective-permute-start | bytes 393224 | tf_op jit(solution)/shard_map/ppermute | solution.py:21
  24.2 33.2 %collective-permute-start.1 = (bf16[64,1024]{1,0:T(8,128)(2,1)}, bf16[64,1024]{1,0:T(8,128)(2,1)S(1)}, u32[]{:S(2)}, u32[]{:S(2)}) collective-permute-start(bf16[64,1024]{1,0:T(8,128)(2,1)} %copy.40), channel_id=1, source_target_pairs={{1,0},{4,1},{5,4},{8,5},{9,8},{12,9},{13,12},{3,2},{6,3},{7,6},{10... | collective-permute-start | bytes 393224 | tf_op jit(solution)/shard_map/ppermute | solution.py:23
  35.6 6.5 %copy-start.17 = (bf16[1024,8,64]{0,2,1:T(8,128)(2,1)S(1)}, bf16[1024,8,64]{0,2,1:T(8,128)(2,1)}, u32[]{:S(2)}) copy-start(bf16[1024,8,64]{0,2,1:T(8,128)(2,1)} %get-tuple-element.16) | copy-start | bytes 3145732
  46.6 111.8 %all-gather.2.cloned.1.call-start = ((), (), s32[]{:S(2)}) async-start(), calls=%async_computation.2 | async-start | bytes 3145728 | tf_op jit(solution)/shard_map/all_gather | solution.py:114
  54.7 2.7 %copy-start.4 = (bf16[1024,1024]{1,0:T(8,128)(2,1)S(1)}, bf16[1024,1024]{1,0:T(8,128)(2,1)}, u32[]{:S(2)}) copy-start(bf16[1024,1024]{1,0:T(8,128)(2,1)} %copy.39) | copy-start | bytes 6291460
  57.1 14.6 %copy-start.9 = (bf16[8,128,8,64]{1,3,2,0:T(8,128)(2,1)}, bf16[8,128,8,64]{1,3,2,0:T(8,128)(2,1)S(1)}, u32[]{:S(2)}) copy-start(bf16[8,128,8,64]{1,3,2,0:T(8,128)(2,1)S(1)} %copy.45) | copy-start | bytes 3145732
  61.2 4.3 %copy-start.5 = (bf16[128,8,8,128]{3,1,2,0:T(8,128)(2,1)S(1)}, bf16[128,8,8,128]{3,1,2,0:T(8,128)(2,1)}, u32[]{:S(2)}) copy-start(bf16[128,8,8,128]{3,1,2,0:T(8,128)(2,1)} %get-tuple-element.11) | copy-start | bytes 6291460
  67.5 4.3 %copy-start.7 = (bf16[8,128,8,128]{1,3,2,0:T(8,128)(2,1)S(1)}, bf16[8,128,8,128]{1,3,2,0:T(8,128)(2,1)}, u32[]{:S(2)}) copy-start(bf16[8,128,8,128]{1,3,2,0:T(8,128)(2,1)} %copy.42) | copy-start | bytes 6291460
  108.6 2.5 %copy-start.10 = (bf16[8,128,8,64]{1,3,2,0:T(8,128)(2,1)S(1)}, bf16[8,128,8,64]{1,3,2,0:T(8,128)(2,1)}, u32[]{:S(2)}) copy-start(bf16[8,128,8,64]{1,3,2,0:T(8,128)(2,1)} %copy-done.9) | copy-start | bytes 3145732
  111.2 9.2 %slice-start = ((s8[8388608]{0:T(1024)(128)(4,1)}), s8[4194304]{0:T(1024)(128)(4,1)S(1)}, s32[]{:S(2)}) async-start(s8[8388608]{0:T(1024)(128)(4,1)} %bitcast.83), calls=%async_computation.4 | async-start | bytes 8388608
  115.2 5.2 %copy-start.8 = (bf16[8,128,8,128]{1,3,2,0:T(8,128)(2,1)S(1)}, bf16[8,128,8,128]{1,3,2,0:T(8,128)(2,1)}, u32[]{:S(2)}) copy-start(bf16[8,128,8,128]{1,3,2,0:T(8,128)(2,1)} %copy.43) | copy-start | bytes 6291460
  115.2 5.2 %slice-start.1 = ((s8[8388608]{0:T(1024)(128)(4,1)}), s8[4194304]{0:T(1024)(128)(4,1)S(1)}, s32[]{:S(2)}) async-start(s8[8388608]{0:T(1024)(128)(4,1)} %bitcast.83), calls=%async_computation.5 | async-start | bytes 8388608
  124.8 1.4 copy-start.14
  124.9 33.5 %copy-start.16 = (bf16[1024,512]{1,0:T(8,128)(2,1)S(1)}, bf16[1024,512]{1,0:T(8,128)(2,1)}, u32[]{:S(2)}) copy-start(bf16[1024,512]{1,0:T(8,128)(2,1)} %param.16) | copy-start | bytes 3145732
  126.1 66.4 %reduce-scatter.2.cloned.1.call-start = ((), (), s32[]{:S(2)}) async-start(), calls=%async_computation.3 | async-start | bytes 73728 | tf_op jit(solution)/shard_map/reduce_scatter | solution.py:128
  158.4 35.6 %copy-start.1 = (bf16[1024,512]{1,0:T(8,128)(2,1)S(1)}, bf16[1024,512]{1,0:T(8,128)(2,1)}, u32[]{:S(2)}) copy-start(bf16[1024,512]{1,0:T(8,128)(2,1)} %param.13) | copy-start | bytes 3145732
  161.4 32.6 %copy-start.11 = (bf16[1024,512]{1,0:T(8,128)(2,1)}, bf16[1024,512]{1,0:T(8,128)(2,1)S(1)}, u32[]{:S(2)}) copy-start(bf16[1024,512]{1,0:T(8,128)(2,1)S(1)} %convolution_convert_fusion) | copy-start | bytes 3145732
  (1 other events, 1.2 us)
Sparse Core Ops, SparseCore 0:
  46.8 60.7 all-reduce.1
  126.3 32.0 all-gather.1
  162.5 30.0 reduce-scatter.1
where the time goes:
time: 201 us; the launch traced here: 200 us
  waiting for transfers between devices  90.6 us (45%)
  matrix products  46.4 us (23%)
  local copies, waits for them, and re-layouts  31.1 us (15%)
  between operations  14.2 us (7%)
  other arithmetic  14 us (7%)
  starting transfers between devices  4.17 us (2%)
    all_gather x1, waiting for transfers between devices, per_device(): lax.all_gather(heads_out, 'head', axis=1, tiled=True)  32.1 us
    reduce_scatter x1, waiting for transfers between devices, per_device(): lax.psum_scatter(partial_sums.astype(jnp.bfloat16), ('seq', 'rep'), scatt...  30.2 us
    psum x1, waiting for transfers between devices, per_device(): lax.psum(numerator.astype(jnp.bfloat16), ('seq', 'rep')).astype(jnp.float32)  28.3 us
    dot_general x1, matrix products, per_device(): logits = jnp.dot(normed, proj_weight, preferred_element_type=jnp.float32)  9.95 us
    slice x2, local copies, waits for them, and re-layouts, per_device(): window = jnp.concatenate([blocks[:-1], blocks[1:]], axis=1)  8.56 us
    dot_general x1, matrix products, per_device(): jnp.einsum('sqhd,skhd->shqk', query_blocks, window[..., :DH], preferred_e...  7.46 us
    unnamed x43, local copies, waits for them, and re-layouts  6.76 us
    reshape x1, local copies, waits for them, and re-layouts, per_device(): jnp.exp(capped(logits)).astype(jnp.bfloat16)  6.49 us
  transfers between devices with their start and end apart: 5, of which 3 were waited for; matrix products, arithmetic and copies ran while one was open for 27% of the time, Pallas kernels for 0%

commit v1 on v0

--- a/solution.py
+++ b/solution.py
@@ -94,7 +94,9 @@
         "sqhd,skhd->shqk", query_blocks, window[..., :DH], preferred_element_type=jnp.float32
     )
     near_exp = jnp.where(inside[:, None, None, :], jnp.exp(capped(near_scores * DH ** (-0.5))), 0.0)
-    total_numer = lax.psum(numerator.astype(jnp.bfloat16), ("seq", "rep")).astype(jnp.float32)
+    total_numer = lax.psum(lax.psum(numerator.astype(jnp.bfloat16), "rep"), "seq").astype(
+        jnp.float32
+    )
     land_pairs = finish(total_numer, gain_rows)
     far_scores = jnp.einsum(
         "sqhd,hrd->shqr", query_blocks, land_pairs[..., :DH], preferred_element_type=jnp.float32

time: 201 us -> 209 us (1.040)
  waiting for transfers between devices: 90.6 us -> 98.7 us
    psum x1 -> x2, waiting for transfers between devices: 28.3 us -> 35.4 us  [the longest x1 35.4 us: per_device(): lax.psum(lax.psum(numerator.astype(jnp.bfloat16), 'rep'), 'seq')]
  transfers between devices with their start and end apart: 5 -> 6, of which waited for: 3 -> 3; matrix products, arithmetic and copies ran while one was open for 27% -> 26% of each run, Pallas kernels for 0% -> 0%
where the time goes in v1:
time: 209 us
  waiting for transfers between devices  98.7 us (47%)
  matrix products  46.4 us (22%)
  local copies, waits for them, and re-layouts  31.1 us (15%)
  between operations  14.2 us (7%)
  other arithmetic  14 us (7%)
  starting transfers between devices  4.21 us (2%)
    psum x1, waiting for transfers between devices, per_device(): lax.psum(lax.psum(numerator.astype(jnp.bfloat16), 'rep'), 'seq')  35.4 us
    all_gather x1, waiting for transfers between devices, per_device(): lax.all_gather(heads_out, 'head', axis=1, tiled=True)  33.1 us
    reduce_scatter x1, waiting for transfers between devices, per_device(): lax.psum_scatter(partial_sums.astype(jnp.bfloat16), ('seq', 'rep'), scatt...  30.2 us
    dot_general x1, matrix products, per_device(): logits = jnp.dot(normed, proj_weight, preferred_element_type=jnp.float32)  9.95 us
    slice x2, local copies, waits for them, and re-layouts, per_device(): window = jnp.concatenate([blocks[:-1], blocks[1:]], axis=1)  8.57 us
    dot_general x1, matrix products, per_device(): jnp.einsum('sqhd,skhd->shqk', query_blocks, window[..., :DH], preferred_e...  7.45 us
    unnamed x43, local copies, waits for them, and re-layouts  6.76 us
    reshape x1, local copies, waits for them, and re-layouts, per_device(): jnp.exp(capped(logits)).astype(jnp.bfloat16)  6.49 us
  transfers between devices with their start and end apart: 6, of which 3 were waited for; matrix products, arithmetic and copies ran while one was open for 26% of the time, Pallas kernels for 0%

profile of v1, /device:TPU:0, one launch (start us, length us, event | category | flops | bytes accessed | tf_op | source)
XLA Modules:
  0.0 208.6 jit_solution(6272047725489434920)
XLA Ops:
  7.2 2.1 convert_reduce_fusion
  10.9 2.3 %bitcast_convert_fusion = (bf16[1024,8,64]{0,2,1:T(8,128)(2,1)}, f32[1024,512]{0,1:T(8,128)S(1)}) fusion(bf16[1024,1024]{1,0:T(8,128)(2,1)S(1)} %fusion.6, bf16[1024,512]{1,0:T(8,128)(2,1)S(1)} %copy-done), kind=kOutput, calls=%fused_computation.34 | convolution fusion | flops 1074266112 | bytes 6291456 | tf_op jit(solution)/shard_map/dot_general | solution.py:69
  14.4 2.3 %bitcast_convert_fusion.1 = (bf16[1024,8,64]{0,2,1:T(8,128)(2,1)}, f32[1024,512]{0,1:T(8,128)S(1)}) fusion(bf16[1024,1024]{1,0:T(8,128)(2,1)S(1)} %fusion.6, bf16[1024,512]{1,0:T(8,128)(2,1)S(1)} %copy-done.15), kind=kOutput, calls=%fused_computation.37 | convolution fusion | flops 1074266112 | bytes 6291456 | tf_op jit(solution)/shard_map/dot_general | solution.py:66
  18.3 2.2 %multiply_multiply_fusion = (bf16[1024,8,64]{0,2,1:T(8,128)(2,1)S(1)}, bf16[1024,8,64]{0,2,1:T(8,128)(2,1)S(1)}) fusion(f32[1024,512]{0,1:T(8,128)S(1)} %get-tuple-element.17, f32[8,64]{1,0:T(8,128)S(1)} %mul.128, f32[1024,8]{0,1:T(8,128)S(1)} %add_rsqrt_fusion, f32[1024,8]{0,1:T(8,128)S(1)} %broadcast_multiply_fusion, f32[8,64]{1,0:T(8,128)S(1)} %mul.123, ...), kind=kLoop, calls=%fused_computation.40 | loop fusion | flops 4194304 | bytes 6426624 | tf_op jit(solution)/shard_map/mul | solution.py:33
  21.0 2.4 %collective-permute-start = (bf16[64,1024]{1,0:T(8,128)(2,1)S(1)}, bf16[64,1024]{1,0:T(8,128)(2,1)S(1)}, u32[]{:S(2)}, u32[]{:S(2)}) collective-permute-start(bf16[64,1024]{1,0:T(8,128)(2,1)S(1)} %copy.38), channel_id=1, source_target_pairs={{0,1},{1,4},{4,5},{5,8},{8,9},{9,12},{12,13},{2,3},{3,6},{6,7},{7,... | collective-permute-start | bytes 393224 | tf_op jit(solution)/shard_map/ppermute | solution.py:21
  25.7 10.0 %exponential_convert_fusion = bf16[1024,2048]{1,0:T(8,128)(2,1)} fusion(bf16[1024,1024]{1,0:T(8,128)(2,1)} %copy-done.6, bf16[1024,2048]{1,0:T(8,128)(2,1)} %param.14), kind=kOutput, calls=%fused_computation.5 | convolution fusion | flops 4301258752 | bytes 10485760 | tf_op jit(solution)/shard_map/dot_general | solution.py:78
  35.6 6.5 %copy.58 = bf16[1024,2048]{0,1:T(8,128)(2,1)} copy(bf16[1024,2048]{1,0:T(8,128)(2,1)} %exponential_convert_fusion) | data formatting | bytes 8388608 | tf_op jit(solution)/shard_map/reshape | solution.py:79
  42.1 4.5 %fusion.23 = bf16[8,256,128]{2,1,0:T(8,128)(2,1)} fusion(bf16[1024,8,256]{0,2,1:T(8,128)(2,1)} %bitcast.78, bf16[1024,8,64]{0,2,1:T(8,128)(2,1)S(1)} %copy-done.17, bf16[1024,8,64]{0,2,1:T(8,128)(2,1)} %get-tuple-element.18), kind=kOutput, calls=%fused_computation.46 | convolution fusion | flops 541327360 | bytes 6815744 | tf_op jit(solution)/shard_map/nhr,nhe->hre/dot_general | solution.py:80
  46.7 2.6 %copy.39 = bf16[1024,1024]{1,0:T(8,128)(2,1)} copy(bf16[1024,1024]{0,1:T(8,128)(2,1)S(1)} %bitcast.75) | data formatting | bytes 4194304 | tf_op jit(solution)/shard_map/convert_element_type | solution.py:76
  49.3 3.1 %convolution_convert_fusion.1 = bf16[1024,512]{1,0:T(8,128)(2,1)S(1)} fusion(bf16[1024,1024]{1,0:T(8,128)(2,1)} %copy-done.6, bf16[1024,512]{1,0:T(8,128)(2,1)} %param.11), kind=kOutput, calls=%fused_computation.45 | convolution fusion | flops 1074266112 | bytes 4194304 | tf_op jit(solution)/shard_map/dot_general | solution.py:64
  52.4 2.1 reshape.140
  54.5 2.4 %copy.45 = bf16[8,128,8,64]{1,3,2,0:T(8,128)(2,1)S(1)} copy(bf16[8,128,8,64]{3,2,1,0:T(8,128)(2,1)} %reshape.140) | data formatting | bytes 2097152 | tf_op jit(solution)/shard_map/reshape;reshape | solution.py:92
  59.1 2.0 copy.64
  61.0 4.3 %copy.42 = bf16[8,128,8,128]{1,3,2,0:T(8,128)(2,1)} copy(bf16[8,128,8,128]{3,2,1,0:T(8,128)(2,1)} %bitcast.76) | data formatting | bytes 4194304 | tf_op jit(solution)/shard_map/slice | solution.py:87
  65.3 1.9 copy.65
  67.3 4.3 %copy.43 = bf16[8,128,8,128]{1,3,2,0:T(8,128)(2,1)} copy(bf16[8,128,8,128]{3,2,1,0:T(8,128)(2,1)} %bitcast.77) | data formatting | bytes 4194304 | tf_op jit(solution)/shard_map/slice | solution.py:87
  71.9 7.5 %fusion.1 = (f32[8,8,128]{2,1,0:T(8,128)S(1)}, f32[8,8,128,256]{3,2,1,0:T(8,128)}) fusion(pred[8,256]{1,0:T(8,128)(4,1)S(1)} %fusion.45, bf16[8,128,8,64]{1,3,2,0:T(8,128)(2,1)S(1)} %copy.45, bf16[8,128,8,128]{1,3,2,0:T(8,128)(2,1)} %copy.43, bf16[8,128,8,128]{1,3,2,0:T(8,128)(2,1)S(1)} %copy-done.7), kind=kOutput, calls=%fused_computation.7 | convolution fusion | flops 281010176 | bytes 13666304 | tf_op jit(solution)/shard_map/sqhd,skhd->shqk/dot_general | solution.py:93
  79.3 35.4 %all-reduce.5.cloned.1.call-done = bf16[8,256,128]{2,1,0:T(8,128)(2,1)} async-done(((bf16[8,256,128]{2,1,0:T(8,128)(2,1)}), bf16[8,256,128]{2,1,0:T(8,128)(2,1)}) %all-reduce.5.cloned.1.call-update) | async-done | bytes 524304 | tf_op jit(solution)/shard_map/psum | solution.py:97
  118.3 3.9 %bitcast_reduce_fusion = (f32[8,8,128]{2,1,0:T(8,128)S(1)}, f32[8,256,8,128]{1,3,0,2:T(8,128)S(1)}) fusion(bf16[8,128,8,64]{1,3,2,0:T(8,128)(2,1)S(1)} %copy-done.10, f32[8,256,128]{2,1,0:T(8,128)S(1)} %convert_element_type.57, f32[8,64]{1,0:T(8,128)S(1)} %mul.138, f32[8,256]{1,0:T(8,128)S(1)} %add_rsqrt_fusion.3, f32[8,256]{1,0:T(8,128)S(1)} %get-tuple-element.25), kind=kOutput, calls=%fused_computation.1 | convolution fusion | flops 275243008 | bytes 10536960 | tf_op jit(solution)/shard_map/sqhd,hrd->shqr/dot_general | solution.py:101
  122.3 5.2 %fusion.8 = f32[8,64,8,128]{3,1,0,2:T(8,128)S(1)} fusion(f32[8,256,8,128]{1,3,0,2:T(8,128)S(1)} %get-tuple-element.23, f32[8,8,128]{2,1,0:T(8,128)S(1)} %add.120, f32[8,256,128]{2,1,0:T(8,128)S(1)} %convert_element_type.57, f32[8,64]{1,0:T(8,128)S(1)} %mul.144, f32[8,256]{1,0:T(8,128)S(1)} %add_rsqrt_fusion.2, f32[8,256]{1,0:T(8,128)S(1)} %get-tuple-element.24), kind=kOutput, calls=%fused_computation.19 | convolution fusion | flops 277348352 | bytes 11585536 | tf_op jit(solution)/shard_map/shqr,hrd->sqhd/dot_general | solution.py:111
  127.5 3.8 %fusion.20 = bf16[8,128,8,64]{1,3,2,0:T(8,128)(2,1)S(1)} fusion(f32[8,64,8,128]{3,1,0,2:T(8,128)S(1)} %fusion.8, f32[8,8,128,256]{3,2,1,0:T(8,128)S(1)} %bitcast.84, f32[8,8,128]{2,1,0:T(8,128)S(1)} %add.120, pred[8,256]{1,0:T(8,128)(4,1)S(1)} %fusion.45, bf16[8,128,8,128]{1,3,2,0:T(8,128)(2,1)S(1)} %copy-done.7, bf16[8,128,8,128]{1,3,2,0:T(8,128)(2,1)S(1)} %copy-done.8), kind=kOutput, calls=%fused_computation.33 | convolution fusion | flops 284164096 | bytes 15763456 | tf_op jit(solution)/shard_map/shqk,skhd->sqhd/dot_general | solution.py:108
  133.4 33.1 %all-gather.2.cloned.1.call-done = bf16[1024,1024]{0,1:T(8,128)(2,1)} async-done(((bf16[1024,512]{0,1:T(8,128)(2,1)}), bf16[1024,1024]{0,1:T(8,128)(2,1)}) %all-gather.2.cloned.1.call-update) | async-done | bytes 2097168 | tf_op jit(solution)/shard_map/all_gather | solution.py:116
  166.5 3.0 %convolution_convert_fusion = bf16[1024,512]{1,0:T(8,128)(2,1)S(1)} fusion(bf16[1024,1024]{0,1:T(8,128)(2,1)} %all-gather.2.cloned.1.call-done, bf16[1024,512]{1,0:T(8,128)(2,1)S(1)} %copy-done.16), kind=kOutput, calls=%fused_computation.44 | convolution fusion | flops 1074266112 | bytes 4194304 | tf_op jit(solution)/shard_map/dot_general | solution.py:115
  170.5 30.2 %reduce-scatter.2.cloned.1.call-done = bf16[8,512]{1,0:T(8,128)(2,1)} async-done(((bf16[64,512]{1,0:T(8,128)(2,1)}), bf16[8,512]{1,0:T(8,128)(2,1)}) %reduce-scatter.2.cloned.1.call-update) | async-done | bytes 8208 | tf_op jit(solution)/shard_map/reduce_scatter | solution.py:130
  (92 shorter events, 17.7 us)
Async XLA Ops:
  7.2 3.7 %copy-start = (bf16[1024,512]{1,0:T(8,128)(2,1)S(1)}, bf16[1024,512]{1,0:T(8,128)(2,1)}, u32[]{:S(2)}) copy-start(bf16[1024,512]{1,0:T(8,128)(2,1)} %param.13) | copy-start | bytes 3145732
  7.2 2.3 %copy-start.2 = (bf16[1024,1024]{1,0:T(8,128)(2,1)S(1)}, bf16[1024,1024]{1,0:T(8,128)(2,1)}, u32[]{:S(2)}) copy-start(bf16[1024,1024]{1,0:T(8,128)(2,1)} %param.9) | copy-start | bytes 6291460
  7.2 3.0 %copy-start.13 = (f32[1024]{0:T(1024)S(1)}, f32[1024]{0:T(1024)}, u32[]{:S(2)}) copy-start(f32[1024]{0:T(1024)} %param.10) | copy-start | bytes 12292
  7.2 64.3 %all-reduce.3.cloned.1.call-start = ((), (), s32[]{:S(2)}) async-start(), calls=%async_computation.1 | async-start | bytes 1048576 | tf_op jit(solution)/shard_map/psum | solution.py:97
  10.9 2.9 %copy-start.6 = (bf16[1024,1024]{1,0:T(8,128)(2,1)}, bf16[1024,1024]{1,0:T(8,128)(2,1)S(1)}, u32[]{:S(2)}) copy-start(bf16[1024,1024]{1,0:T(8,128)(2,1)S(1)} %fusion.6) | copy-start | bytes 6291460
  16.7 1.4 copy-start.12
  21.0 36.1 %collective-permute-start = (bf16[64,1024]{1,0:T(8,128)(2,1)S(1)}, bf16[64,1024]{1,0:T(8,128)(2,1)S(1)}, u32[]{:S(2)}, u32[]{:S(2)}) collective-permute-start(bf16[64,1024]{1,0:T(8,128)(2,1)S(1)} %copy.38), channel_id=1, source_target_pairs={{0,1},{1,4},{4,5},{5,8},{8,9},{9,12},{12,13},{2,3},{3,6},{6,7},{7,... | collective-permute-start | bytes 393224 | tf_op jit(solution)/shard_map/ppermute | solution.py:21
  24.2 33.0 %collective-permute-start.1 = (bf16[64,1024]{1,0:T(8,128)(2,1)}, bf16[64,1024]{1,0:T(8,128)(2,1)S(1)}, u32[]{:S(2)}, u32[]{:S(2)}) collective-permute-start(bf16[64,1024]{1,0:T(8,128)(2,1)} %copy.40), channel_id=1, source_target_pairs={{1,0},{4,1},{5,4},{8,5},{9,8},{12,9},{13,12},{3,2},{6,3},{7,6},{10... | collective-permute-start | bytes 393224 | tf_op jit(solution)/shard_map/ppermute | solution.py:23
  35.6 6.5 %copy-start.17 = (bf16[1024,8,64]{0,2,1:T(8,128)(2,1)S(1)}, bf16[1024,8,64]{0,2,1:T(8,128)(2,1)}, u32[]{:S(2)}) copy-start(bf16[1024,8,64]{0,2,1:T(8,128)(2,1)} %get-tuple-element.16) | copy-start | bytes 3145732
  46.7 68.0 %all-reduce.5.cloned.1.call-start = ((), (), s32[]{:S(2)}) async-start(), calls=%async_computation.2 | async-start | bytes 1048576 | tf_op jit(solution)/shard_map/psum | solution.py:97
  54.5 2.7 %copy-start.4 = (bf16[1024,1024]{1,0:T(8,128)(2,1)S(1)}, bf16[1024,1024]{1,0:T(8,128)(2,1)}, u32[]{:S(2)}) copy-start(bf16[1024,1024]{1,0:T(8,128)(2,1)} %copy.39) | copy-start | bytes 6291460
  56.9 14.9 %copy-start.9 = (bf16[8,128,8,64]{1,3,2,0:T(8,128)(2,1)}, bf16[8,128,8,64]{1,3,2,0:T(8,128)(2,1)S(1)}, u32[]{:S(2)}) copy-start(bf16[8,128,8,64]{1,3,2,0:T(8,128)(2,1)S(1)} %copy.45) | copy-start | bytes 3145732
  61.0 4.3 %copy-start.5 = (bf16[128,8,8,128]{3,1,2,0:T(8,128)(2,1)S(1)}, bf16[128,8,8,128]{3,1,2,0:T(8,128)(2,1)}, u32[]{:S(2)}) copy-start(bf16[128,8,8,128]{3,1,2,0:T(8,128)(2,1)} %get-tuple-element.11) | copy-start | bytes 6291460
  67.2 4.6 %copy-start.7 = (bf16[8,128,8,128]{1,3,2,0:T(8,128)(2,1)S(1)}, bf16[8,128,8,128]{1,3,2,0:T(8,128)(2,1)}, u32[]{:S(2)}) copy-start(bf16[8,128,8,128]{1,3,2,0:T(8,128)(2,1)} %copy.42) | copy-start | bytes 6291460
  71.6 95.0 %all-gather.2.cloned.1.call-start = ((), (), s32[]{:S(2)}) async-start(), calls=%async_computation.3 | async-start | bytes 3145728 | tf_op jit(solution)/shard_map/all_gather | solution.py:116
  115.8 2.5 %copy-start.10 = (bf16[8,128,8,64]{1,3,2,0:T(8,128)(2,1)S(1)}, bf16[8,128,8,64]{1,3,2,0:T(8,128)(2,1)}, u32[]{:S(2)}) copy-start(bf16[8,128,8,64]{1,3,2,0:T(8,128)(2,1)} %copy-done.9) | copy-start | bytes 3145732
  118.3 9.2 %slice-start = ((s8[8388608]{0:T(1024)(128)(4,1)}), s8[4194304]{0:T(1024)(128)(4,1)S(1)}, s32[]{:S(2)}) async-start(s8[8388608]{0:T(1024)(128)(4,1)} %bitcast.83), calls=%async_computation.5 | async-start | bytes 8388608
  122.3 5.2 %copy-start.8 = (bf16[8,128,8,128]{1,3,2,0:T(8,128)(2,1)S(1)}, bf16[8,128,8,128]{1,3,2,0:T(8,128)(2,1)}, u32[]{:S(2)}) copy-start(bf16[8,128,8,128]{1,3,2,0:T(8,128)(2,1)} %copy.43) | copy-start | bytes 6291460
  122.3 5.2 %slice-start.1 = ((s8[8388608]{0:T(1024)(128)(4,1)}), s8[4194304]{0:T(1024)(128)(4,1)S(1)}, s32[]{:S(2)}) async-start(s8[8388608]{0:T(1024)(128)(4,1)} %bitcast.83), calls=%async_computation.6 | async-start | bytes 8388608
  132.0 1.4 copy-start.14
  132.0 34.5 %copy-start.16 = (bf16[1024,512]{1,0:T(8,128)(2,1)S(1)}, bf16[1024,512]{1,0:T(8,128)(2,1)}, u32[]{:S(2)}) copy-start(bf16[1024,512]{1,0:T(8,128)(2,1)} %param.16) | copy-start | bytes 3145732
  133.3 67.4 %reduce-scatter.2.cloned.1.call-start = ((), (), s32[]{:S(2)}) async-start(), calls=%async_computation.4 | async-start | bytes 73728 | tf_op jit(solution)/shard_map/reduce_scatter | solution.py:130
  166.5 35.6 %copy-start.1 = (bf16[1024,512]{1,0:T(8,128)(2,1)S(1)}, bf16[1024,512]{1,0:T(8,128)(2,1)}, u32[]{:S(2)}) copy-start(bf16[1024,512]{1,0:T(8,128)(2,1)} %param.13) | copy-start | bytes 3145732
  169.5 32.6 %copy-start.11 = (bf16[1024,512]{1,0:T(8,128)(2,1)}, bf16[1024,512]{1,0:T(8,128)(2,1)S(1)}, u32[]{:S(2)}) copy-start(bf16[1024,512]{1,0:T(8,128)(2,1)S(1)} %convolution_convert_fusion) | copy-start | bytes 3145732
  (2 other events, 2.6 us)
Sparse Core Ops, SparseCore 0:
  46.8 23.3 all-reduce.2
  72.6 41.9 all-reduce.4
  133.4 33.0 all-gather.1
  170.7 30.0 reduce-scatter.1
